TPU v7x, 32 devices: a whole 2x2x4 slice. The times are simulated.
32 devices in a mesh: dp: 4 (over y, core), ctx: 2 (over x), mp: 4 (over z).
Axes of the slice: x: 2, y: 2, z: 4, core: 2. Of those that a mesh axis runs over, the one named last changes fastest.
Arguments:
- block_input: bfloat16 [4, 1024, 2048], P('dp', 'ctx'), may hold values from -40 to 40
- norm_one_gain: bfloat16 [2048], P(('dp', 'ctx')), may hold values from 0.5 to 1.5
- query_weight: bfloat16 [2048, 3072], P(('dp', 'ctx'), 'mp'), may hold values from -0.125 to 0.125
- latent_weight: bfloat16 [2048, 576], P(('dp', 'ctx')), may hold values from -0.125 to 0.125
- latent_gain: bfloat16 [512], P(('dp', 'ctx')), may hold values from 0.5 to 1.5
- expand_weight: bfloat16 [512, 4096], P(('dp', 'ctx'), 'mp'), may hold values from -0.25 to 0.25
- output_weight: bfloat16 [2048, 2048], P('mp', ('dp', 'ctx')), may hold values from -0.5 to 0.5
- norm_two_gain: bfloat16 [2048], P(('dp', 'ctx')), may hold values from 0.5 to 1.5
- router_weight: bfloat16 [2048, 8], P(('dp', 'ctx')), may hold values from -0.25 to 0.25
- expert_gate: bfloat16 [8, 2048, 1408], P('mp', ('dp', 'ctx')), may hold values from -0.125 to 0.125
- expert_up: bfloat16 [8, 2048, 1408], P('mp', ('dp', 'ctx')), may hold values from -0.125 to 0.125
- expert_down: bfloat16 [8, 1408, 2048], P('mp', None, ('dp', 'ctx')), may hold values from -0.15625 to 0.15625
- shared_gate: bfloat16 [2048, 2816], P(('dp', 'ctx'), 'mp'), may hold values from -0.125 to 0.125
- shared_up: bfloat16 [2048, 2816], P(('dp', 'ctx'), 'mp'), may hold values from -0.125 to 0.125
- shared_down: bfloat16 [2816, 2048], P('mp', ('dp', 'ctx')), may hold values from -0.109375 to 0.109375
- routes: int32 [4, 1024, 6], P('dp', 'ctx'), may hold values from 0 to 7, as said below
- route_slots: int32 [4, 1024, 6], P('dp', 'ctx'), may hold values from 0 to 511, as said below
- cotangent: bfloat16 [4, 1024, 2048], P('dp', 'ctx'), may hold values from -6 to 6
Outputs:
- block_output: bfloat16 [4, 1024, 2048], P('dp', 'ctx')
- input_grad: bfloat16 [4, 1024, 2048], P('dp', 'ctx')
- norm_one_gain_grad: float32 [2048], P(('dp', 'ctx'))
- query_weight_grad: float32 [2048, 3072], P(('dp', 'ctx'), 'mp')
- latent_weight_grad: float32 [2048, 576], P(('dp', 'ctx'))
- latent_gain_grad: float32 [512], P(('dp', 'ctx'))
- expand_weight_grad: float32 [512, 4096], P(('dp', 'ctx'), 'mp')
- output_weight_grad: float32 [2048, 2048], P('mp', ('dp', 'ctx'))
- norm_two_gain_grad: float32 [2048], P(('dp', 'ctx'))
- router_weight_grad: float32 [2048, 8], P(('dp', 'ctx'))
- expert_gate_grad: float32 [8, 2048, 1408], P('mp', ('dp', 'ctx'))
- expert_up_grad: float32 [8, 2048, 1408], P('mp', ('dp', 'ctx'))
- expert_down_grad: float32 [8, 1408, 2048], P('mp', None, ('dp', 'ctx'))
- shared_gate_grad: float32 [2048, 2816], P(('dp', 'ctx'), 'mp')
- shared_up_grad: float32 [2048, 2816], P(('dp', 'ctx'), 'mp')
- shared_down_grad: float32 [2816, 2048], P('mp', ('dp', 'ctx'))
Inputs may be any that keep to these rules, and one draw needn't show every extreme that they name: `routes`: each token names 6 different experts. Among the tokens of one group (one index of dp and of ctx) some expert is named by every token. `route_slots`: among the tokens of one group (one index of dp and of ctx), each pair of expert and slot is named at most once.
All inputs are finite; a program needn't handle non-finite values.
Results may differ from a plain program's by a relative error of at most 0.025.
Values may be sent and summed in bfloat16 or wider, within the bound.
No kernel may reach another device: no remote copies, remote signals or barrier semaphores. Data moves between devices by JAX's collectives and lax.ppermute only.
A program may use at most 208 MiB of HBM per device.

v0:
```python
import jax
import jax.numpy as jnp
from jax import lax
from jax.experimental import pallas as pl
from jax.experimental.pallas import tpu as pltpu
from jax.sharding import PartitionSpec as P


D = 2048
QN = 128
QR = 64
VD = 128
KVR = 512
TOP = 6
LANES = 128
EPSILON = 1e-06
LAT, EXPAND, OUTPUT, QUERY, SHARED, DOWN, SDOWN, GATE, UP = "012345678"
ONE, TWO, THREE, FOUR, FIVE = "abcde"
F32 = jnp.float32
BF16 = jnp.bfloat16


def dot_nn(left_in, right_in):
    return lax.dot_general(left_in, right_in, (((1,), (0,)), ((), ())), preferred_element_type=F32)


def dot_tn(left_in, right_in):
    return lax.dot_general(left_in, right_in, (((0,), (0,)), ((), ())), preferred_element_type=F32)


def dot_nt(left_in, right_in):
    return lax.dot_general(left_in, right_in, (((1,), (1,)), ((), ())), preferred_element_type=F32)


def norm_rows(values, gain_vec):
    inverse = lax.rsqrt(jnp.mean(values * values, axis=-1, keepdims=True) + EPSILON)
    normed = values * inverse
    return (normed * gain_vec, normed, inverse)


def norm_back(grad_out, normed, inverse, gain_vec):
    scaled = grad_out * gain_vec
    grad_in = inverse * (scaled - normed * jnp.mean(normed * scaled, axis=-1, keepdims=True))
    return (grad_in, jnp.sum(grad_out * normed, axis=0))


def rotate(values, cosines, sines):
    half_dim = values.shape[-1] // 2
    first_half = values[..., :half_dim]
    second_half = values[..., half_dim:]
    return jnp.concatenate(
        [first_half * cosines - second_half * sines, second_half * cosines + first_half * sines],
        axis=-1,
    )


def bytes_of(*arrays):
    return sum(v.size * v.dtype.itemsize for v in arrays)


def cost(flops, moved, exps=0):
    return pl.CostEstimate(flops=flops, transcendentals=exps, bytes_accessed=moved)


def tile_of(count, parts):
    while parts > 1 and (count % parts or (count // parts) % 16):
        parts -= 1
    return count // parts


def column_blocks(order, values):
    rows, cols = values.shape
    width = cols // 8
    tile = tile_of(rows, 4)

    def body(order_ref, in_ref, out_ref):
        for i in range(8):
            start = pl.multiple_of(order_ref[i] * width, width)
            out_ref[:, i * width : (i + 1) * width] = in_ref[:, pl.ds(start, width)]

    spec = pl.BlockSpec((tile, cols), lambda i, order_ref: (i, 0))
    return pl.pallas_call(
        body,
        out_shape=jax.ShapeDtypeStruct(values.shape, values.dtype),
        grid_spec=pltpu.PrefetchScalarGridSpec(
            num_scalar_prefetch=1, grid=(rows // tile,), in_specs=[spec], out_specs=spec
        ),
        cost_estimate=cost(0, 2 * bytes_of(values)),
    )(order, values)


def row_blocks(order, values):
    rows = values.shape[0] // 8

    def body(order_ref, in_ref, out_ref):
        for i in range(8):
            start = pl.multiple_of(order_ref[i] * rows, rows)
            out_ref[i * rows : (i + 1) * rows, :] = in_ref[pl.ds(start, rows), :]

    spec = pl.BlockSpec(values.shape, lambda i, order_ref: (0, 0))
    return pl.pallas_call(
        body,
        out_shape=jax.ShapeDtypeStruct(values.shape, values.dtype),
        grid_spec=pltpu.PrefetchScalarGridSpec(
            num_scalar_prefetch=1, grid=(1,), in_specs=[spec], out_specs=spec
        ),
        cost_estimate=cost(0, 2 * bytes_of(values)),
    )(order, values)


def place_rows(order, pieces):
    rows, cols = pieces[0].shape
    count = len(pieces)

    def body(order_ref, *refs):
        for i in range(count):
            start = pl.multiple_of(order_ref[i] * rows, rows)
            refs[count][pl.ds(start, rows), :] = refs[i][...]

    return pl.pallas_call(
        body,
        out_shape=jax.ShapeDtypeStruct((count * rows, cols), pieces[0].dtype),
        grid_spec=pltpu.PrefetchScalarGridSpec(
            num_scalar_prefetch=1,
            grid=(1,),
            in_specs=[pl.BlockSpec((rows, cols), lambda i, order_ref: (0, 0))] * count,
            out_specs=pl.BlockSpec((count * rows, cols), lambda i, order_ref: (0, 0)),
        ),
        cost_estimate=cost(0, 2 * bytes_of(*pieces)),
    )(order, *pieces)


def arrivals(group):
    return 0 if group["x_first"] else 1


def add_three(groups, last, total):
    count = len(groups)
    cols = last[0].shape[1]
    axis, size = groups[0]["axis"], groups[0]["size"]
    tile = tile_of(total, 4)
    specs = []
    for g in groups:
        skip = arrivals(g) * (size // tile) if axis == 0 else 0
        side = arrivals(g) if axis == 1 else 0
        specs.append(pl.BlockSpec((tile, cols), lambda i: (i, 0)))
        specs.append(pl.BlockSpec((tile, cols), lambda i, skip=skip, side=side: (i + skip, side)))
        specs.append(pl.BlockSpec((tile, cols), lambda i: (i, 0)))

    def body(*refs):
        for e in range(count):
            held, here, after = (refs[3 * e + k][...].astype(F32) for k in range(3))
            refs[3 * count][e] = held + here + after

    return pl.pallas_call(
        body,
        out_shape=jax.ShapeDtypeStruct((count, total, cols), F32),
        grid=(total // tile,),
        in_specs=specs,
        out_specs=pl.BlockSpec((count, tile, cols), lambda i: (0, i, 0)),
        cost_estimate=cost(3 * count * total * cols, 10 * count * total * cols),
    )(*[v for g, w in zip(groups, last) for v in (g["held"], g["near"], w)])


def add_three_turned(group, last, columns):
    rows, cols = last.shape
    side = arrivals(group)
    spec = pl.BlockSpec((rows, cols), lambda i: (0, 0))

    def body(held_ref, here_ref, last_ref, *out_refs):
        for ref, (start, count) in zip(out_refs, columns):
            part = slice(start, start + count)
            total = held_ref[:, part].astype(F32) + here_ref[:, part].astype(F32)
            ref[...] = (total + last_ref[:, part].astype(F32)).T

    return pl.pallas_call(
        body,
        out_shape=[jax.ShapeDtypeStruct((n, rows), F32) for _, n in columns],
        grid=(1,),
        in_specs=[spec, pl.BlockSpec((rows, cols), lambda i: (side, 0)), spec],
        out_specs=[pl.BlockSpec((n, rows), lambda i: (0, 0)) for _, n in columns],
        cost_estimate=cost(3 * rows * cols, 10 * rows * cols),
    )(group["held"], group["near"], last)


def join_columns(pieces):
    rows, width = pieces[0].shape
    count = len(pieces)
    tile = tile_of(rows, max(2, bytes_of(*pieces) >> 20))

    def body(*refs):
        for i in range(count):
            refs[count][:, i * width : (i + 1) * width] = refs[i][...]

    return pl.pallas_call(
        body,
        out_shape=jax.ShapeDtypeStruct((rows, count * width), pieces[0].dtype),
        grid=(rows // tile,),
        in_specs=[pl.BlockSpec((tile, width), lambda i: (i, 0))] * count,
        out_specs=pl.BlockSpec((tile, count * width), lambda i: (i, 0)),
        cost_estimate=cost(0, 2 * bytes_of(*pieces)),
    )(*pieces)


def join_rows(pieces, count, joined=None):
    experts, rows, cols = pieces[0].shape
    given = len(pieces)
    tile = tile_of(rows, max(2, bytes_of(*pieces) >> 20))
    shape = jax.ShapeDtypeStruct((count, rows, cols), pieces[0].dtype)
    if joined is None:
        places = [i for i in range(count) if given == count or i % 4 != 2]

        def body(*refs):
            for e in range(experts):
                for ref, place in zip(refs, places):
                    refs[given + e][place] = ref[e]

        out = pl.pallas_call(
            body,
            out_shape=[shape] * experts,
            grid=(rows // tile,),
            in_specs=[pl.BlockSpec((experts, tile, cols), lambda i: (0, i, 0))] * given,
            out_specs=[pl.BlockSpec((count, tile, cols), lambda i: (0, i, 0))] * experts,
            cost_estimate=cost(0, 2 * bytes_of(*pieces)),
        )(*pieces)
        return [v.reshape(count * rows, cols) for v in out]
    whole = [v.reshape(given, count // given, rows, cols) for v in joined]

    def fill(*refs):
        for e in range(experts):
            for i in range(given):
                refs[given + experts + e][i, 0] = refs[i][e]

    out = pl.pallas_call(
        fill,
        out_shape=[jax.ShapeDtypeStruct(v.shape, v.dtype) for v in whole],
        grid=(rows // tile,),
        in_specs=[pl.BlockSpec((experts, tile, cols), lambda i: (0, i, 0))] * given
        + [pl.BlockSpec(memory_space=pl.ANY)] * experts,
        out_specs=[pl.BlockSpec((given, 1, tile, cols), lambda i: (0, 2, i, 0))] * experts,
        input_output_aliases={given + e: e for e in range(experts)},
        cost_estimate=cost(0, 2 * bytes_of(*pieces)),
    )(*pieces, *whole)
    return [v.reshape(count * rows, cols) for v in out]


def pick_of(head, heads):
    half = QR // 2
    row = lax.broadcasted_iota(jnp.int32, (QR, heads * QR), 0)
    lane = lax.broadcasted_iota(jnp.int32, (QR, heads * QR), 1)
    place = (row // half) * (heads * half) + head * half + row % half
    return jnp.where(lane == place, 1.0, 0.0).astype(BF16)


def attend(plain, turned, pairs, rope, query_pos, key_pos, seqs, heads):
    span = plain.shape[0] // seqs
    keys = pairs.shape[0] // seqs
    scale = (QN + QR) ** (-0.5)
    rope_cols = heads * QR

    def body(plain_ref, turned_ref, pairs_ref, rope_ref, qpos_ref, kpos_ref, probs_ref, out_ref):
        turned_own = dot_nt(turned_ref[...], pick_of(pl.program_id(1), heads)).astype(BF16)
        logits = dot_nt(plain_ref[...], pairs_ref[:, :QN]) + dot_nt(turned_own, rope_ref[...])
        seen = qpos_ref[...] >= kpos_ref[...]
        exps = jnp.where(seen, jnp.exp(logits * scale), 0.0)
        probs = (exps / jnp.sum(exps, axis=-1, keepdims=True)).astype(BF16)
        probs_ref[0] = probs
        out_ref[...] = dot_nn(probs, pairs_ref[:, QN:]).astype(BF16)

    return pl.pallas_call(
        body,
        out_shape=(
            jax.ShapeDtypeStruct((seqs * heads, span, keys), BF16),
            jax.ShapeDtypeStruct((seqs * span, heads * VD), BF16),
        ),
        grid=(seqs, heads),
        in_specs=[
            pl.BlockSpec((span, QN), lambda s, h: (s, h)),
            pl.BlockSpec((span, rope_cols), lambda s, h: (s, 0)),
            pl.BlockSpec((keys, QN + VD), lambda s, h: (s, h)),
            pl.BlockSpec((keys, QR), lambda s, h: (s, 0)),
            pl.BlockSpec((span, 1), lambda s, h: (0, 0)),
            pl.BlockSpec((1, keys), lambda s, h: (0, 0)),
        ],
        out_specs=(
            pl.BlockSpec((1, span, keys), lambda s, h: (s * heads + h, 0, 0)),
            pl.BlockSpec((span, VD), lambda s, h: (s, h)),
        ),
        cost_estimate=cost(
            2 * seqs * heads * span * keys * (QN + rope_cols + VD),
            bytes_of(plain, turned, pairs) + 2 * seqs * heads * span * keys,
            seqs * heads * span * keys,
        ),
    )(plain, turned, pairs, rope, query_pos[:, None], key_pos[None, :])


def attend_back(plain, turned, pairs, rope, probs, grad_heads, seqs, heads):
    span = plain.shape[0] // seqs
    keys = pairs.shape[0] // seqs
    scale = (QN + QR) ** (-0.5)
    rope_cols = heads * QR

    def body(
        plain_ref, turned_ref, pairs_ref, rope_ref, probs_ref, grad_ref,
        dplain_ref, dturned_ref, dpairs_ref, drope_ref,
    ):
        head = pl.program_id(1)
        pick = pick_of(head, heads)
        turned_own = dot_nt(turned_ref[...], pick).astype(BF16)
        probs_low = probs_ref[0]
        probs_f = probs_low.astype(F32)
        grad = grad_ref[...]
        grad_probs = dot_nt(grad, pairs_ref[:, QN:])
        delta = jnp.sum(probs_f * grad_probs, axis=-1, keepdims=True)
        grad_logits = (probs_f * (grad_probs - delta) * scale).astype(BF16)
        dplain_ref[...] = dot_nn(grad_logits, pairs_ref[:, :QN]).astype(BF16)
        dpairs_ref[:, QN:] = dot_tn(probs_low, grad).astype(BF16)
        dpairs_ref[:, :QN] = dot_tn(grad_logits, plain_ref[...]).astype(BF16)
        turned_part = dot_nn(dot_nn(grad_logits, rope_ref[...]).astype(BF16), pick)
        rope_part = dot_tn(grad_logits, turned_own)

        @pl.when(head == 0)
        def _():
            dturned_ref[...] = turned_part
            drope_ref[...] = rope_part

        @pl.when(head > 0)
        def _():
            dturned_ref[...] += turned_part
            drope_ref[...] += rope_part

    return pl.pallas_call(
        body,
        out_shape=(
            jax.ShapeDtypeStruct(plain.shape, BF16),
            jax.ShapeDtypeStruct(turned.shape, F32),
            jax.ShapeDtypeStruct(pairs.shape, BF16),
            jax.ShapeDtypeStruct(rope.shape, F32),
        ),
        grid=(seqs, heads),
        in_specs=[
            pl.BlockSpec((span, QN), lambda s, h: (s, h)),
            pl.BlockSpec((span, rope_cols), lambda s, h: (s, 0)),
            pl.BlockSpec((keys, QN + VD), lambda s, h: (s, h)),
            pl.BlockSpec((keys, QR), lambda s, h: (s, 0)),
            pl.BlockSpec((1, span, keys), lambda s, h: (s * heads + h, 0, 0)),
            pl.BlockSpec((span, VD), lambda s, h: (s, h)),
        ],
        out_specs=(
            pl.BlockSpec((span, QN), lambda s, h: (s, h)),
            pl.BlockSpec((span, rope_cols), lambda s, h: (s, 0)),
            pl.BlockSpec((keys, QN + VD), lambda s, h: (s, h)),
            pl.BlockSpec((keys, QR), lambda s, h: (s, 0)),
        ),
        cost_estimate=cost(
            2 * seqs * heads * span * keys * (2 * QN + 2 * VD + 2 * QR),
            2 * bytes_of(plain, turned, pairs) + bytes_of(probs),
        ),
    )(plain, turned, pairs, rope, probs, grad_heads)


def pad_cols(values, width):
    return jnp.pad(values, ((0, 0), (0, width - values.shape[1])))


def up_to(count, step):
    return -(-count // step) * step


class Plan:
    def __init__(self, sizes):
        self.dp = sizes["dp"]
        self.ctx = sizes["ctx"]
        self.fast = self.dp == 4 and self.ctx == 2
        if self.fast:
            me = lax.axis_index("dp") * 2 + lax.axis_index("ctx")
            ids = jnp.arange(8, dtype=jnp.int32)
            y, core, x = (ids >> 1) & 1, ids >> 2, (ids ^ (ids >> 1)) & 1
            self.order = ((4 * y + 2 * core + x) ^ me).astype(jnp.int32)
            apart = ids ^ me
            y, core, x = apart >> 2, (apart >> 1) & 1, apart & 1
            self.inverse = (4 * core + x + y * (3 - 2 * x)).astype(jnp.int32)

    @staticmethod
    def over_core(values):
        return lax.ppermute(values, "dp", [(i, i ^ 1) for i in range(4)])

    @staticmethod
    def over_y(values):
        return lax.ppermute(values, "dp", [(i, i ^ 2) for i in range(4)])

    @staticmethod
    def over_x(values):
        return lax.ppermute(values, "ctx", [(0, 1), (1, 0)])

    def tie(self, values, *after):
        return lax.optimization_barrier((values, after))[0] if self.fast else values

    def to_own(self, values):
        return column_blocks(self.order, values) if self.fast else values

    def to_natural(self, values):
        return column_blocks(self.inverse, values) if self.fast else values

    def spread(self, shard):
        if not self.fast:
            return ()
        return (self.over_x(shard), self.over_y(shard))

    def collect(self, name, shard, near, axis, x_last, *after):
        if not self.fast:
            full = lax.all_gather(shard, ("dp", "ctx"), axis=axis, tiled=True)
            return (list(full), lambda *after: list(full)) if shard.ndim == 3 else full
        from_x, from_y = near
        from_xy = self.over_x(from_y) if x_last else self.over_y(from_x)
        own = [shard, from_x, from_xy, from_y]
        if shard.ndim == 3:
            early = self.tie([shard, from_x, from_y], *after)
            early = early + [self.over_core(v) for v in early]
            joined = join_rows(early, 8)

            def rest(*after):
                late = self.tie(from_xy, joined, *after)
                late = [late, self.over_core(late)]
                return join_rows(late, 8, joined)

            return joined, rest
        own[2] = self.tie(from_xy, *after)
        pieces = own + [self.over_core(v) for v in own]
        if name == EXPAND:
            return place_rows(self.order, pieces)
        if axis == 0:
            return join_rows([v[None] for v in pieces], 8)[0]
        return join_columns(pieces)

    def over(self, values, first, x_first):
        return self.over_x(values) if first == x_first else self.over_y(values)

    def begin(self, name, left_in, right_in, size, axis, x_first):
        if not self.fast:
            return self.begin_given(name, dot_tn(left_in, right_in).astype(BF16), size, axis, x_first)
        half = 4 * size

        def part(a, b):
            if axis == 0:
                return dot_tn(left_in[:, a:b], right_in)
            return dot_tn(left_in, right_in[:, a:b])

        sent = self.over_core(part(half, 2 * half).astype(BF16))
        held = (part(0, half) + sent.astype(F32)).astype(BF16)
        return {"held": held, "x_first": x_first, "name": name, "size": size, "axis": axis}

    def cut(self, group, name, i, count=1):
        size = group["size"]
        return lax.slice_in_dim(group[name], i * size, (i + count) * size, axis=group["axis"])

    def begin_given(self, name, whole, size, axis, x_first):
        if not self.fast:
            held = lax.psum_scatter(whole, ("dp", "ctx"), scatter_dimension=axis, tiled=True)
        else:
            sent = self.over_core(lax.slice_in_dim(whole, 4 * size, 8 * size, axis=axis))
            held = lax.slice_in_dim(whole, 0, 4 * size, axis=axis).astype(F32)
            held = (held + sent.astype(F32)).astype(BF16)
        return {"held": held, "x_first": x_first, "name": name, "size": size, "axis": axis}

    def first(self, groups):
        if not self.fast:
            return
        for g in groups:
            both = self.cut(g, "held", 1 if g["x_first"] else 2, 2)
            g["near"] = self.over(both, True, g["x_first"])

    def second(self, groups, *after):
        if not self.fast:
            return
        near = self.tie([g["near"] for g in groups], *after)
        for g, v in zip(groups, near):
            g["near"] = v
            kept = self.cut(g, "held", 3 if g["x_first"] else 1).astype(F32)
            there = self.cut(g, "near", 1 if g["x_first"] else 0).astype(F32)
            g["last"] = self.over((kept + there).astype(BF16), False, g["x_first"])

    def finish(self, groups, rows, *after):
        if not self.fast:
            return jnp.stack([g["held"][:rows].astype(F32) for g in groups])
        last = self.tie([g["last"] for g in groups], *after)
        return add_three(groups, last, rows)

    def finish_turned(self, group, columns, *after):
        if not self.fast:
            return [group["held"][:, a : a + n].astype(F32) for a, n in columns]
        last = self.tie(group["last"], *after)
        return [v.T for v in add_three_turned(group, last, columns)]


def scatter_mp(values, n_mp, direct, tie):
    if not direct:
        return lax.psum_scatter(values, "mp", scatter_dimension=0, tiled=True).astype(F32)
    share = values.shape[0] // n_mp
    me = lax.axis_index("mp")

    def part(i):
        return lax.dynamic_slice_in_dim(values, (i % n_mp) * share, share, axis=0)

    arrived = []
    for step in range(1, n_mp):
        path = [(i, (i + step) % n_mp) for i in range(n_mp)]
        arrived.append(lax.ppermute(part(me + step), "mp", path))
    return sum((v.astype(F32) for v in tie(arrived)), part(me).astype(F32))


def gather_mp(values, n_mp, direct, tie):
    if not direct:
        return lax.all_gather(values, "mp", axis=0, tiled=True)
    share = values.shape[0]
    me = lax.axis_index("mp")
    others = [values]
    for step in range(1, n_mp):
        path = [(i, (i + step) % n_mp) for i in range(n_mp)]
        others.append(lax.ppermute(values, "mp", path))
    whole = jnp.zeros((n_mp * share,) + values.shape[1:], values.dtype)
    for step, other in enumerate(tie(others)):
        whole = lax.dynamic_update_slice_in_dim(
            whole, other, ((me - step) % n_mp) * share, axis=0
        )
    return whole


def sum_mp(values, n_mp):
    total = values
    for step in range(1, n_mp):
        path = [(i, (i + step) % n_mp) for i in range(n_mp)]
        total = total + lax.ppermute(values, "mp", path)
    return total


def local(
    sizes,
    block_input,
    norm_one_gain,
    query_weight,
    latent_weight,
    latent_gain,
    expand_weight,
    output_weight,
    norm_two_gain,
    router_weight,
    expert_gate,
    expert_up,
    expert_down,
    shared_gate,
    shared_up,
    shared_down,
    routes,
    route_slots,
    cotangent,
):
    plan = Plan(sizes)
    fast = plan.fast
    n_mp = sizes["mp"]
    mp_index = lax.axis_index("mp")
    seq_count, span_len = block_input.shape[0], block_input.shape[1]
    rows = seq_count * span_len
    shard_rows = rows // n_mp
    head_dim = QN + QR
    q_cols = query_weight.shape[1]
    local_heads = q_cols // head_dim
    experts_here = expert_gate.shape[0]
    experts_all = router_weight.shape[1]
    hidden = expert_gate.shape[2]
    shared_cols = shared_gate.shape[1]
    shared_pad = up_to(shared_cols, 2 * LANES)
    block = norm_one_gain.shape[0]
    rank_block = expand_weight.shape[0]

    half_dim = QR // 2
    both_halves = local_heads * half_dim

    if fast:
        gains = jnp.concatenate([norm_one_gain, norm_two_gain, latent_gain]).astype(F32)[None]
        gains_x = plan.over_x(gains)
        gains = jnp.concatenate([gains, gains_x], axis=0)
        gains_y = plan.over_y(gains)
        gains = jnp.concatenate([gains, gains_y[1:], gains_y[:1]], axis=0)
        gains_core = plan.over_core(gains)
        gains = jnp.concatenate([gains, gains_core], axis=0)
        gain_one = gains[:, :block].reshape(8 * block)
        gain_two = gains[:, block : 2 * block].reshape(8 * block)
        rank_rel = gains[:, 2 * block :]
        place = (plan.inverse[:, None] == jnp.arange(8, dtype=jnp.int32)[None, :]).astype(F32)
        gain_latent = jnp.sum(place[:, :, None] * rank_rel[None, :, :], axis=1).reshape(KVR)
    latent_cols = KVR + QR
    latent_shard = jnp.concatenate([latent_weight, router_weight], axis=1)
    latent_near = plan.spread(latent_shard)
    expand_near = plan.spread(expand_weight)
    output_near = plan.spread(output_weight)
    query_weight = plan.tie(query_weight, *latent_near)
    by_head = query_weight.reshape(block, local_heads, head_dim)
    query_shard = jnp.concatenate(
        [
            by_head[:, :, :QN].reshape(block, local_heads * QN),
            by_head[:, :, QN : QN + half_dim].reshape(block, both_halves),
            by_head[:, :, QN + half_dim :].reshape(block, both_halves),
        ],
        axis=1,
    )
    query_near = plan.spread(query_shard)
    latent_router = plan.collect(LAT, latent_shard, latent_near, 0, True)
    latent_full = latent_router[:, :latent_cols]
    router_full = latent_router[:, latent_cols:]
    if not fast:
        gain_one = lax.all_gather(norm_one_gain, ("dp", "ctx"), tiled=True).astype(F32)
        gain_two = lax.all_gather(norm_two_gain, ("dp", "ctx"), tiled=True).astype(F32)
        gain_latent = lax.all_gather(latent_gain, ("dp", "ctx"), tiled=True).astype(F32)

    ctx_index = lax.axis_index("ctx")
    frequencies = 10000.0 ** (-jnp.arange(half_dim, dtype=F32) / half_dim)
    steps = jnp.arange(span_len, dtype=jnp.int32)
    query_pos = ctx_index * span_len + steps
    angles = jnp.tile(query_pos.astype(F32)[:, None] * frequencies[None, :], (seq_count, 1))
    cosines = jnp.cos(angles)
    sines = jnp.sin(angles)
    lanes = jnp.arange(both_halves, dtype=jnp.int32) % half_dim
    all_frequencies = 10000.0 ** (-lanes.astype(F32) / half_dim)
    all_angles = jnp.tile(query_pos.astype(F32), seq_count)[:, None] * all_frequencies[None, :]
    cos_heads = jnp.cos(all_angles)
    sin_heads = jnp.sin(all_angles)

    row_start = mp_index * shard_rows

    def own_rows(values):
        return lax.dynamic_slice_in_dim(values, row_start, shard_rows, axis=0)

    x_low = plan.to_own(block_input.reshape(rows, D))
    x_own = own_rows(x_low).astype(F32)
    h_one = norm_rows(x_low.astype(F32), gain_one)[0].astype(BF16)
    latent = dot_nn(h_one, latent_router)[:, :latent_cols]
    comp_f = norm_rows(latent[:, :KVR], gain_latent)[0]
    key_rope = rotate(latent[:, KVR:], cosines, sines)
    shared_kv = jnp.concatenate([comp_f, key_rope], axis=1).astype(BF16)

    shared_kv = shared_kv.reshape(seq_count, span_len, KVR + QR)
    if plan.ctx == 2:
        other_kv = plan.over_x(shared_kv)
        kv_all = jnp.concatenate([shared_kv, other_kv], axis=1)
        key_pos = jnp.concatenate([query_pos, (1 - ctx_index) * span_len + steps])
    else:
        kv_all = lax.all_gather(shared_kv, "ctx", axis=1, tiled=True)
        key_pos = jnp.arange(plan.ctx * span_len, dtype=jnp.int32)
    down_shards = [expert_down[e] for e in range(experts_here)]
    down_shards = plan.tie(down_shards, shared_kv)
    down_near = [plan.spread(v) for v in down_shards]
    gate_shard = plan.tie(expert_gate, shared_kv)
    gate_near = plan.spread(gate_shard)

    query_near, expand_near, output_near = (
        plan.tie(v, shared_kv) for v in (query_near, expand_near, output_near)
    )
    query_full = plan.collect(QUERY, query_shard, query_near, 0, False)
    expand_full = plan.collect(EXPAND, expand_weight, expand_near, 0, False)
    output_full = plan.collect(OUTPUT, output_weight, output_near, 1, True)
    seq_len = key_pos.shape[0]
    comp_all = kv_all[..., :KVR].reshape(seq_count * seq_len, KVR)
    rope_all = kv_all[..., KVR:].reshape(seq_count * seq_len, QR)
    q_raw = dot_nn(h_one, query_full)
    plain_cols = local_heads * QN
    plain = q_raw[:, :plain_cols].astype(BF16)
    first = q_raw[:, plain_cols : plain_cols + both_halves]
    second = q_raw[:, plain_cols + both_halves :]
    turned = jnp.concatenate(
        [first * cos_heads - second * sin_heads, second * cos_heads + first * sin_heads], axis=1
    ).astype(BF16)
    pairs = dot_nn(comp_all, expand_full).astype(BF16)
    probs, heads_flat = attend(
        plain, turned, pairs, rope_all, query_pos, key_pos, seq_count, local_heads
    )
    attn_part = dot_nn(heads_flat, output_full).astype(BF16)
    attn_sum = lax.psum_scatter(attn_part, "mp", scatter_dimension=0, tiled=True)

    cotangent, route_rows, slot_rows = plan.tie(
        (cotangent, routes.reshape(rows, TOP), route_slots.reshape(rows, TOP)), attn_part
    )
    g_low = plan.to_own(cotangent.reshape(rows, D))
    g_own = own_rows(g_low).astype(F32)
    slot_ids = jnp.arange(rows, dtype=jnp.int32)
    hits = []
    for e in range(experts_here):
        named = route_rows == mp_index * experts_here + e
        slot = jnp.sum(jnp.where(named, slot_rows + 1, 0), axis=-1) - 1
        hits.append(slot[:, None] == slot_ids[None, :])
    one_hot = [v.astype(BF16) for v in hits]
    both_hot = jnp.concatenate(one_hot, axis=1)
    g_slots = [dot_tn(v, g_low).astype(BF16) for v in one_hot]
    down_near = [plan.tie(v, attn_part) for v in down_near]
    down_full = [plan.collect(DOWN, down_shards[0], down_near[0], 1, True, *g_slots)]
    act_back = [dot_nt(g_slots[0], down_full[0]).astype(BF16)]
    attn_sum = plan.tie(attn_sum, act_back, *g_slots)
    up_shard = plan.tie(expert_up, attn_part)
    up_near = plan.spread(up_shard)
    shared_gate, shared_up, shared_down = plan.tie((shared_gate, shared_up, shared_down), *g_slots)
    shared_shard = jnp.concatenate(
        [pad_cols(shared_gate, shared_pad), pad_cols(shared_up, shared_pad)], axis=1
    )
    sdown_shard = jnp.pad(shared_down, ((0, shared_pad - shared_cols), (0, 0)))
    shared_near = plan.spread(shared_shard)
    sdown_near = plan.spread(sdown_shard)

    mixed = x_own + attn_sum.astype(F32)
    h_two_f, normed_two, inverse_two = norm_rows(mixed, gain_two)
    h_two_own = h_two_f.astype(BF16)
    h_two = lax.all_gather(h_two_own, "mp", axis=0, tiled=True)

    gate_near = plan.tie(gate_near, h_two_own)
    gate_joined, gate_rest = plan.collect(GATE, gate_shard, gate_near, 1, True)
    up_near = plan.tie(up_near, gate_joined)
    up_joined, up_rest = plan.collect(UP, up_shard, up_near, 1, False)
    after = up_joined
    for e in range(1, experts_here):
        full = plan.collect(DOWN, down_shards[e], down_near[e], 1, e % 2 == 0, after)
        down_full.append(full)
        act_back.append(dot_nt(g_slots[e], full).astype(BF16))
        after = act_back[e]
    gate_full = gate_rest(after)

    dispatched = [dot_tn(v, h_two).astype(BF16) for v in one_hot]
    gate_all = plan.tie([dot_nn(dispatched[e], gate_full[e]) for e in range(experts_here)])
    up_full = up_rest(gate_all)
    router_exp = jnp.exp(dot_nn(h_two, router_full))
    router_probs = router_exp / jnp.sum(router_exp, axis=-1, keepdims=True)
    probs_here = lax.dynamic_slice_in_dim(router_probs, mp_index * experts_here, experts_here, 1)
    slot_gate = [
        jnp.sum(jnp.where(hits[e], probs_here[:, e : e + 1], 0.0), axis=0)
        for e in range(experts_here)
    ]
    grad_gates, grad_ups, act_gated, slot_grads = [], [], [], []
    for e in range(experts_here):
        gate_vals = gate_all[e]
        up_vals = dot_nn(dispatched[e], up_full[e])
        sig = jax.nn.sigmoid(gate_vals)
        act = gate_vals * sig * up_vals
        gated = slot_gate[e][:, None]
        back = act_back[e].astype(F32)
        slot_grads.append(jnp.sum(back * act, axis=-1))
        back = back * gated
        grad_gate = (back * up_vals * sig * (1.0 + gate_vals * (1.0 - sig))).astype(BF16)
        grad_up = (back * gate_vals * sig).astype(BF16)
        grad_gate, grad_up, act = plan.tie((grad_gate, grad_up, (act * gated).astype(BF16)))
        grad_gates.append(grad_gate)
        grad_ups.append(grad_up)
        act_gated.append(act)


    shared_near, sdown_near = plan.tie((shared_near, sdown_near), h_two_own)
    shared_full = plan.collect(SHARED, shared_shard, shared_near, 0, False, act_gated)
    sdown_full = plan.collect(SDOWN, sdown_shard, sdown_near, 1, True, shared_full)
    shared_back = dot_nt(g_low, sdown_full)
    shared_vals = dot_nn(h_two, shared_full)
    shared_a = shared_vals[:, :shared_pad]
    shared_b = shared_vals[:, shared_pad:]
    shared_sig = jax.nn.sigmoid(shared_a)
    shared_act = (shared_a * shared_sig * shared_b).astype(BF16)
    grad_shared_gate = shared_back * shared_b * shared_sig * (1.0 + shared_a * (1.0 - shared_sig))
    grad_shared_up = shared_back * shared_a * shared_sig
    grad_shared = jnp.concatenate([grad_shared_gate, grad_shared_up], axis=1).astype(BF16)

    grad_slots = []
    for e in range(experts_here):
        grad_slot = dot_nt(grad_gates[e], gate_full[e]) + dot_nt(grad_ups[e], up_full[e])
        grad_slots.append(grad_slot.astype(BF16))
    grad_h_two = dot_nn(both_hot, jnp.concatenate(grad_slots, axis=0)) + dot_nt(
        grad_shared, shared_full
    )
    expert_ids = jnp.arange(LANES, dtype=jnp.int32)
    grad_probs_part = jnp.zeros((rows, LANES), F32)
    for e in range(experts_here):
        of_token = jnp.sum(jnp.where(hits[e], slot_grads[e][None, :], 0.0), axis=1)
        grad_probs_part = grad_probs_part + jnp.where(
            expert_ids[None, :] == mp_index * experts_here + e, of_token[:, None], 0.0
        )
    back_part = jnp.concatenate([grad_h_two.astype(BF16), grad_probs_part.astype(BF16)], axis=1)
    back_sum = lax.psum_scatter(back_part, "mp", scatter_dimension=0, tiled=True).astype(F32)

    acts, slots_g, acts_s, g_late, h_late, shared_late = plan.tie(
        (act_gated, g_slots, shared_act, g_low, h_two, grad_shared), back_part
    )
    sums_one = [
        plan.begin(ONE, h_late, shared_late, block, 0, False),
        plan.begin(ONE, acts_s, g_late, block, 1, True),
    ] + [
        plan.begin(ONE, acts[e], slots_g[e], block, 1, e % 2 == 0)
        for e in range(experts_here)
    ]
    plan.first(sums_one)
    back_sum = plan.tie(back_sum, *[g["held"] for g in sums_one])

    probs_own = own_rows(router_probs)
    grad_probs = back_sum[:, D : D + experts_all]
    grad_logits = (
        probs_own * (grad_probs - jnp.sum(probs_own * grad_probs, axis=-1, keepdims=True))
    ).astype(BF16)
    grad_two = back_sum[:, :D] + dot_nt(grad_logits, router_full)
    grad_norm, norm_two_part = norm_back(grad_two, normed_two, inverse_two, gain_two)
    grad_mixed = g_own + grad_norm
    mixed_part = jnp.concatenate([grad_mixed.astype(BF16), pad_cols(grad_logits, LANES)], axis=1)
    mixed_all = lax.all_gather(mixed_part, "mp", axis=0, tiled=True)

    acts_out, shared_act_out = plan.tie((act_gated, shared_act), mixed_part)
    expert_out = [dot_nn(acts_out[e], down_full[e]).astype(BF16) for e in range(experts_here)]
    ff_part = dot_nn(both_hot, jnp.concatenate(expert_out, axis=0)) + dot_nn(
        shared_act_out, sdown_full
    )
    ff_part = ff_part.astype(BF16)
    ff_sum = lax.psum_scatter(ff_part, "mp", scatter_dimension=0, tiled=True).astype(F32)


    sent_rows, gates_late = plan.tie((dispatched, grad_gates), mixed_part)
    sums_two = [
        plan.begin(TWO, sent_rows[e], gates_late[e], block, 0, e % 2 == 0)
        for e in range(experts_here)
    ]
    plan.first(sums_two)
    mixed_all = plan.tie(mixed_all, *[g["held"] for g in sums_two])

    grad_low = mixed_all[:, :D]
    grad_heads = dot_nt(grad_low, output_full).astype(BF16)
    dplain, dturned, grad_pairs, grad_rope = attend_back(
        plain, turned, pairs, rope_all, probs, grad_heads, seq_count, local_heads
    )
    back_first = dturned[:, :both_halves]
    back_second = dturned[:, both_halves:]
    grad_q_raw = jnp.concatenate(
        [
            dplain,
            (back_first * cos_heads + back_second * sin_heads).astype(BF16),
            (back_second * cos_heads - back_first * sin_heads).astype(BF16),
        ],
        axis=1,
    )
    query_part = dot_nt(grad_q_raw, query_full).astype(BF16)
    grad_one = lax.psum_scatter(query_part, "mp", scatter_dimension=0, tiled=True).astype(F32)
    grad_comp = dot_nt(grad_pairs, expand_full).reshape(seq_count, seq_len, KVR)
    grad_rope = grad_rope.reshape(seq_count, seq_len, QR)
    grad_kv = jnp.concatenate([grad_comp, grad_rope], axis=-1)
    if plan.ctx == 2:
        to_other = grad_kv[:, span_len:].astype(BF16)
        from_other = plan.over_x(to_other)
        grad_kv = grad_kv[:, :span_len] + from_other.astype(F32)
    else:
        to_other = ()
        grad_kv = grad_kv.reshape(seq_count, plan.ctx, span_len, KVR + QR).transpose(1, 0, 2, 3)
        grad_kv = grad_kv.reshape(plan.ctx * rows, KVR + QR).astype(BF16)
        grad_kv = lax.psum_scatter(grad_kv, "ctx", scatter_dimension=0, tiled=True)
    sent_late, ups_late = plan.tie((dispatched, grad_ups), query_part, to_other)
    plan.second(sums_one, query_part, to_other)
    plan.second(sums_two, query_part, to_other)
    sums_three = [
        plan.begin(THREE, sent_late[e], ups_late[e], block, 0, e % 2 == 1)
        for e in range(experts_here)
    ]
    plan.first(sums_three)
    grad_kv = scatter_mp(
        grad_kv.reshape(rows, KVR + QR).astype(BF16),
        n_mp,
        fast,
        lambda values: plan.tie(values, *[g["held"] for g in sums_three]),
    )
    _, comp_normed, comp_inverse = norm_rows(own_rows(latent)[:, :KVR], gain_latent)
    grad_comp_in, latent_gain_part = norm_back(
        grad_kv[:, :KVR], comp_normed, comp_inverse, gain_latent
    )
    grad_latent = jnp.concatenate(
        [grad_comp_in, rotate(grad_kv[:, KVR:], own_rows(cosines), -own_rows(sines))], axis=1
    ).astype(BF16)
    grad_one = grad_one + dot_nt(grad_latent, latent_full)
    _, normed_one, inverse_one = norm_rows(x_own, gain_one)
    grad_tokens, norm_one_part = norm_back(grad_one, normed_one, inverse_one, gain_one)
    input_own = plan.to_natural((grad_mixed + grad_tokens).astype(BF16))
    input_grad = lax.all_gather(input_own, "mp", axis=0, tiled=True)

    result_own = plan.to_natural((mixed + ff_sum).astype(BF16))
    result_own = plan.tie(result_own, mixed_all)
    result = lax.all_gather(result_own, "mp", axis=0, tiled=True)

    h_tail, heads_tail, low_tail, q_tail, comp_tail, pairs_tail = plan.tie(
        (h_one, heads_flat, grad_low, grad_q_raw, comp_all, grad_pairs), input_own
    )
    sums_four = [
        plan.begin(FOUR, heads_tail, low_tail, block, 1, True),
        plan.begin(FOUR, h_tail, q_tail, block, 0, False),
    ]
    expand_whole = dot_tn(comp_tail, pairs_tail).astype(BF16)
    if fast:
        expand_whole = row_blocks(plan.order, expand_whole)
    sums_four.append(plan.begin_given(FOUR, expand_whole, rank_block, 0, True))
    plan.first(sums_four)
    held_four = [g["held"] for g in sums_four]
    plan.second(sums_three)
    sgate_grad, sup_grad = plan.finish_turned(
        sums_one[0], [(0, shared_cols), (shared_pad, shared_cols)], held_four
    )
    sdown_grad = plan.finish(sums_one[1:2], shared_cols, held_four)[0]
    down_grads = plan.finish(sums_one[2:], hidden, held_four)
    gate_grads = plan.finish(sums_two, block, held_four)
    latent_all = gather_mp(grad_latent, n_mp, fast, lambda values: plan.tie(values, held_four))
    plan.second(sums_four)
    sums_five = [plan.begin(FIVE, h_tail, latent_all, block, 0, False)]
    plan.first(sums_five)
    plan.second(sums_five)
    up_grads = plan.finish(sums_three, block, latent_all)
    output_grad, query_grad, expand_grad = (
        plan.finish([g], n, latent_all)[0]
        for g, n in zip(sums_four, (output_weight.shape[0], block, rank_block))
    )
    (latent_grad,) = plan.finish_turned(sums_five[0], [(0, latent_cols)])
    query_grad = jnp.concatenate(
        [
            query_grad[:, :plain_cols].reshape(block, local_heads, QN),
            query_grad[:, plain_cols:][:, :both_halves].reshape(block, local_heads, half_dim),
            query_grad[:, plain_cols + both_halves :].reshape(block, local_heads, half_dim),
        ],
        axis=2,
    ).reshape(block, q_cols)

    router_part = dot_tn(mixed_all[:, D : D + experts_all], h_two)
    if fast:
        to_rel = (plan.order[:, None] == jnp.arange(8, dtype=jnp.int32)[None, :]).astype(F32)
        latent_rel = jnp.sum(
            to_rel[:, :, None] * latent_gain_part.reshape(1, 8, rank_block), axis=1
        )
        router_once = jnp.where(mp_index == 0, router_part, 0.0)
        router_rel = router_once.reshape(experts_all, 8, block).transpose(1, 0, 2)
        small = jnp.concatenate(
            [
                norm_one_part.reshape(8, block),
                norm_two_part.reshape(8, block),
                router_rel.reshape(8, experts_all * block),
                pad_cols(latent_rel, LANES),
            ],
            axis=1,
        )
        small = small[:4] + plan.over_core(small[4:])
        from_y = plan.over_y(small[2:])
        small = small[:2] + jnp.concatenate([from_y[1:], from_y[:1]], axis=0)
        small = small[:1] + plan.over_x(small[1:])
        small = sum_mp(small, n_mp)[0]
        norm_one_grad = small[:block]
        norm_two_grad = small[block : 2 * block]
        router_grad = small[2 * block : (2 + experts_all) * block].reshape(experts_all, block).T
        latent_gain_grad = small[(2 + experts_all) * block :][:rank_block]
    else:

        def scatter(values):
            return lax.psum_scatter(values, ("dp", "ctx"), scatter_dimension=0, tiled=True)

        norm_one_grad = scatter(lax.psum(norm_one_part, "mp"))
        norm_two_grad = scatter(lax.psum(norm_two_part, "mp"))
        latent_gain_grad = scatter(lax.psum(latent_gain_part, "mp"))
        router_grad = scatter(router_part.T)

    return (
        result.reshape(seq_count, span_len, D),
        input_grad.reshape(seq_count, span_len, D),
        norm_one_grad,
        query_grad,
        latent_grad,
        latent_gain_grad,
        expand_grad,
        output_grad,
        norm_two_grad,
        router_grad,
        gate_grads,
        up_grads,
        down_grads,
        sgate_grad,
        sup_grad,
        sdown_grad,
    )


def solution(mesh):
    both = ("dp", "ctx")
    tokens = P("dp", "ctx", None)
    in_specs = (
        tokens,
        P(both),
        P(both, "mp"),
        P(both, None),
        P(both),
        P(both, "mp"),
        P("mp", both),
        P(both),
        P(both, None),
        P("mp", both, None),
        P("mp", both, None),
        P("mp", None, both),
        P(both, "mp"),
        P(both, "mp"),
        P("mp", both),
        tokens,
        tokens,
        tokens,
    )
    out_specs = (tokens,) + in_specs[:1] + in_specs[1:15]
    sizes = dict(mesh.shape)

    def per_device(*args):
        return local(sizes, *args)

    return jax.shard_map(
        per_device, mesh=mesh, in_specs=in_specs, out_specs=out_specs, check_vma=False
    )
```

profile of v0, /device:TPU:0, one launch (start us, length us, event | category | flops | bytes accessed | tf_op | source)
XLA Modules:
  0.0 923.9 jit_solution(9400041009937971480)
XLA Ops:
  66.1 9.1 collective-permute-done.20.refs_2_
  103.4 9.7 %shard_map.301 = (bf16[4,512,1024]{2,1,0:T(8,128)(2,1)}, bf16[512,512]{1,0:T(8,128)(2,1)}) custom-call(bf16[512,512]{1,0:T(8,128)(2,1)} %slice.702.plain_ref, bf16[512,256]{1,0:T(8,128)(2,1)} %pad_maximum_fusion.9.turned_ref, bf16[1024,1024]{1,0:T(8,128)(2,1)} %convolution_convert_fusion.17.pairs_ref, bf16[1024,64]{1,0:T(8,128)(2,1)} %maximum_bitcast_fusion.rope_ref, ...), custom_call_target="tpu_custom_call" | custom-call | flops 2147483648 | bytes 7077888 | tf_op jit(solution)/shard_map/pallas_call | solution.py:270
  120.6 16.8 %collective-permute-done.32.refs_1_ = bf16[1408,256]{1,0:T(8,128)(2,1)} collective-permute-done((bf16[1408,256]{1,0:T(8,128)(2,1)S(1)}, bf16[1408,256]{1,0:T(8,128)(2,1)}, u32[]{:S(2)}, u32[]{:S(2)}) %collective-permute-start.32) | collective-permute-done | bytes 720928 | tf_op jit(solution)/shard_map/ppermute | solution.py:394
  174.6 14.8 %collective-permute-done.41.refs_1_ = bf16[2,256,1408]{2,1,0:T(8,128)(2,1)} collective-permute-done((bf16[2,256,1408]{2,1,0:T(8,128)(2,1)}, bf16[2,256,1408]{2,1,0:T(8,128)(2,1)}, u32[]{:S(2)}, u32[]{:S(2)}) %collective-permute-start.41) | collective-permute-done | bytes 1441824 | tf_op jit(solution)/shard_map/ppermute | solution.py:394
  198.3 9.7 %shard_map.305 = (bf16[8,256,1408]{2,1,0:T(8,128)(2,1)}, bf16[8,256,1408]{2,1,0:T(8,128)(2,1)}) custom-call(bf16[2,256,1408]{2,1,0:T(8,128)(2,1)} %refs_0_.4, bf16[2,256,1408]{2,1,0:T(8,128)(2,1)} %collective-permute-done.41.refs_1_, bf16[2,256,1408]{2,1,0:T(8,128)(2,1)} %collective-permute-done.42.refs_2_, ...), custom_call_target="tpu_custom_call" | custom-call | bytes 17301504 | tf_op jit(solution)/shard_map/pallas_call | solution.py:218
  208.0 17.9 %collective-permute-done.39.refs_1_ = bf16[2,256,1408]{2,1,0:T(8,128)(2,1)} collective-permute-done((bf16[2,256,1408]{2,1,0:T(8,128)(2,1)}, bf16[2,256,1408]{2,1,0:T(8,128)(2,1)}, u32[]{:S(2)}, u32[]{:S(2)}) %collective-permute-start.39) | collective-permute-done | bytes 1441824 | tf_op jit(solution)/shard_map/ppermute | solution.py:394
  227.0 13.8 %collective-permute-done.51.refs_1_ = bf16[1408,256]{1,0:T(8,128)(2,1)S(1)} collective-permute-done((bf16[1408,256]{1,0:T(8,128)(2,1)S(1)}, bf16[1408,256]{1,0:T(8,128)(2,1)S(1)}, u32[]{:S(2)}, u32[]{:S(2)}) %collective-permute-start.51) | collective-permute-done | bytes 720928 | tf_op jit(solution)/shard_map/ppermute | solution.py:394
  245.7 9.7 %shard_map.306 = (bf16[8,256,1408]{2,1,0:T(8,128)(2,1)}, bf16[8,256,1408]{2,1,0:T(8,128)(2,1)}) custom-call(bf16[2,256,1408]{2,1,0:T(8,128)(2,1)} %refs_0_.5, bf16[2,256,1408]{2,1,0:T(8,128)(2,1)} %collective-permute-done.39.refs_1_, bf16[2,256,1408]{2,1,0:T(8,128)(2,1)} %collective-permute-done.40.refs_2_, ...), custom_call_target="tpu_custom_call" | custom-call | bytes 17301504 | tf_op jit(solution)/shard_map/pallas_call | solution.py:218
  278.3 18.1 %collective-permute-done.50.refs_0_ = bf16[2,256,1408]{2,1,0:T(8,128)(2,1)} collective-permute-done((bf16[2,256,1408]{2,1,0:T(8,128)(2,1)}, bf16[2,256,1408]{2,1,0:T(8,128)(2,1)}, u32[]{:S(2)}, u32[]{:S(2)}) %collective-permute-start.50) | collective-permute-done | bytes 1441824 | tf_op jit(solution)/shard_map/ppermute | solution.py:394
  307.7 8.4 fusion.162
  321.1 10.0 %collective-permute-done.46.refs_0_ = bf16[2,256,1408]{2,1,0:T(8,128)(2,1)} collective-permute-done((bf16[2,256,1408]{2,1,0:T(8,128)(2,1)}, bf16[2,256,1408]{2,1,0:T(8,128)(2,1)}, u32[]{:S(2)}, u32[]{:S(2)}) %collective-permute-start.46) | collective-permute-done | bytes 1441824 | tf_op jit(solution)/shard_map/ppermute | solution.py:390
  337.7 23.3 %collective-permute-done.62.refs_1_ = bf16[768,256]{1,0:T(8,128)(2,1)S(1)} collective-permute-done((bf16[768,256]{1,0:T(8,128)(2,1)S(1)}, bf16[768,256]{1,0:T(8,128)(2,1)S(1)}, u32[]{:S(2)}, u32[]{:S(2)}) %collective-permute-start.62) | collective-permute-done | bytes 393248 | tf_op jit(solution)/shard_map/ppermute | solution.py:394
  369.4 8.4 fusion.26
  457.0 10.4 %collective-permute-done.75 = bf16[768,1024]{1,0:T(8,128)(2,1)S(1)} collective-permute-done((bf16[768,1024]{1,0:T(8,128)(2,1)S(1)}, bf16[768,1024]{1,0:T(8,128)(2,1)S(1)}, u32[]{:S(2)}, u32[]{:S(2)}) %collective-permute-start.75) | collective-permute-done | bytes 1572896 | tf_op jit(solution)/shard_map/ppermute | solution.py:386
  479.7 13.8 %reduce-scatter.7.cloned.1.call-done = bf16[128,2176]{1,0:T(8,128)(2,1)} async-done(((bf16[512,2176]{1,0:T(8,128)(2,1)}), bf16[128,2176]{1,0:T(8,128)(2,1)}) %reduce-scatter.7.cloned.1.call-update) | async-done | bytes 557072 | tf_op jit(solution)/shard_map/reduce_scatter | solution.py:781
  523.2 34.3 %all-gather.7.cloned.1.call-done = bf16[512,2176]{1,0:T(8,128)(2,1)} async-done(((bf16[128,2176]{1,0:T(8,128)(2,1)}), bf16[512,2176]{1,0:T(8,128)(2,1)}) %all-gather.7.cloned.1.call-update) | async-done | bytes 2228240 | tf_op jit(solution)/shard_map/all_gather | solution.py:805
  561.8 12.8 %shard_map.313 = (bf16[512,512]{1,0:T(8,128)(2,1)}, f32[512,256]{1,0:T(8,128)}, bf16[1024,1024]{1,0:T(8,128)(2,1)}, f32[1024,64]{1,0:T(8,128)}) custom-call(bf16[512,512]{1,0:T(8,128)(2,1)} %slice.702.plain_ref, bf16[512,256]{1,0:T(8,128)(2,1)} %pad_maximum_fusion.9.turned_ref, bf16[1024,1024]{1,0:T(8,128)(2,1)} %convolution_convert_fusion.17.pairs_ref, ...), custom_call_target="tpu_custom_call" | custom-call | flops 2684354560 | bytes 9961472 | tf_op jit(solution)/shard_map/pallas_call | solution.py:332
  628.0 8.2 collective-permute-done.117.refs_1_
  642.8 16.0 %collective-permute-done.115.here_ref = bf16[512,1536]{1,0:T(8,128)(2,1)} collective-permute-done((bf16[512,1536]{1,0:T(8,128)(2,1)}, bf16[512,1536]{1,0:T(8,128)(2,1)}, u32[]{:S(2)}, u32[]{:S(2)}) %collective-permute-start.115) | collective-permute-done | bytes 1572896 | tf_op jit(solution)/shard_map/ppermute | solution.py:390
  763.0 18.0 %collective-permute-done.111.refs_1_ = bf16[512,1408]{1,0:T(8,128)(2,1)S(1)} collective-permute-done((bf16[512,1408]{1,0:T(8,128)(2,1)}, bf16[512,1408]{1,0:T(8,128)(2,1)S(1)}, u32[]{:S(2)}, u32[]{:S(2)}) %collective-permute-start.111) | collective-permute-done | bytes 1441824 | tf_op jit(solution)/shard_map/ppermute | solution.py:390
  792.9 9.8 %collective-permute-done.94.refs_1_ = bf16[512,512]{1,0:T(8,128)(2,1)S(1)} collective-permute-done((bf16[512,512]{1,0:T(8,128)(2,1)S(1)}, bf16[512,512]{1,0:T(8,128)(2,1)S(1)}, u32[]{:S(2)}, u32[]{:S(2)}) %collective-permute-start.94) | collective-permute-done | bytes 524320 | tf_op jit(solution)/shard_map/ppermute | solution.py:394
  825.4 9.8 %collective-permute-done.121.last_ref = bf16[256,1536]{1,0:T(8,128)(2,1)} collective-permute-done((bf16[256,1536]{1,0:T(8,128)(2,1)}, bf16[256,1536]{1,0:T(8,128)(2,1)}, u32[]{:S(2)}, u32[]{:S(2)}) %collective-permute-start.121) | collective-permute-done | bytes 786464 | tf_op jit(solution)/shard_map/ppermute | solution.py:394
  838.3 12.3 %collective-permute-done.110.refs_5_ = bf16[256,1408]{1,0:T(8,128)(2,1)} collective-permute-done((bf16[256,1408]{1,0:T(8,128)(2,1)}, bf16[256,1408]{1,0:T(8,128)(2,1)}, u32[]{:S(2)}, u32[]{:S(2)}) %collective-permute-start.110) | collective-permute-done | bytes 720928 | tf_op jit(solution)/shard_map/ppermute | solution.py:394
  852.0 14.0 %collective-permute-done.113.refs_2_ = bf16[256,1408]{1,0:T(8,128)(2,1)} collective-permute-done((bf16[256,1408]{1,0:T(8,128)(2,1)}, bf16[256,1408]{1,0:T(8,128)(2,1)}, u32[]{:S(2)}, u32[]{:S(2)}) %collective-permute-start.113) | collective-permute-done | bytes 720928 | tf_op jit(solution)/shard_map/ppermute | solution.py:394
  (790 shorter events, 578.4 us)
Async XLA Ops:
  7.2 164.1 %reduce-scatter.5.cloned.1.call-start = ((), (), s32[]{:S(2)}) async-start(), calls=%async_computation.4 | async-start | bytes 2621440 | tf_op jit(solution)/shard_map/reduce_scatter | solution.py:678
  117.5 179.7 %all-gather.5.cloned.1.call-start = ((), (), s32[]{:S(2)}) async-start(), calls=%async_computation.5 | async-start | bytes 2621440 | tf_op jit(solution)/shard_map/all_gather | solution.py:711
  194.2 46.6 %collective-permute-start.51 = (bf16[1408,256]{1,0:T(8,128)(2,1)S(1)}, bf16[1408,256]{1,0:T(8,128)(2,1)S(1)}, u32[]{:S(2)}, u32[]{:S(2)}) collective-permute-start(bf16[1408,256]{1,0:T(8,128)(2,1)S(1)} %get-tuple-element.171.refs_0_), channel_id=1, source_target_pairs={{0,4},{4,0},{1,5},{5,1},{2,6},{6,2},{3,7},{7,3},{8,12},{12,8},{9,1... | collective-permute-start | bytes 2162696 | tf_op jit(solution)/shard_map/ppermute | solution.py:394
  226.9 266.6 %reduce-scatter.7.cloned.1.call-start = ((), (), s32[]{:S(2)}) async-start(), calls=%async_computation.6 | async-start | bytes 2785280 | tf_op jit(solution)/shard_map/reduce_scatter | solution.py:781
  360.9 52.8 %collective-permute-start.65 = (bf16[256,1536]{1,0:T(8,128)(2,1)}, bf16[256,1536]{1,0:T(8,128)(2,1)}, u32[]{:S(2)}, u32[]{:S(2)}) collective-permute-start(bf16[256,1536]{1,0:T(8,128)(2,1)} %get-tuple-element.364), channel_id=1, source_target_pairs={{0,8},{8,0},{16,24},{24,16},{1,9},{9,1},{17,25},{25,17},{2,10},{10... | collective-permute-start | bytes 2359304 | tf_op jit(solution)/shard_map/ppermute | solution.py:386
  362.4 51.8 %collective-permute-start.66 = (bf16[256,1536]{1,0:T(8,128)(2,1)}, bf16[256,1536]{1,0:T(8,128)(2,1)}, u32[]{:S(2)}, u32[]{:S(2)}) collective-permute-start(bf16[256,1536]{1,0:T(8,128)(2,1)} %collective-permute-done.60), channel_id=1, source_target_pairs={{0,8},{8,0},{16,24},{24,16},{1,9},{9,1},{17,25},{25,17},{2,10},{10... | collective-permute-start | bytes 2359304 | tf_op jit(solution)/shard_map/ppermute | solution.py:386
  362.4 51.9 %collective-permute-start.68 = (bf16[256,1536]{1,0:T(8,128)(2,1)}, bf16[256,1536]{1,0:T(8,128)(2,1)}, u32[]{:S(2)}, u32[]{:S(2)}) collective-permute-start(bf16[256,1536]{1,0:T(8,128)(2,1)} %collective-permute-done.61), channel_id=1, source_target_pairs={{0,8},{8,0},{16,24},{24,16},{1,9},{9,1},{17,25},{25,17},{2,10},{10... | collective-permute-start | bytes 2359304 | tf_op jit(solution)/shard_map/ppermute | solution.py:386
  365.4 55.3 %collective-permute-start.69 = (bf16[768,256]{1,0:T(8,128)(2,1)}, bf16[768,256]{1,0:T(8,128)(2,1)}, u32[]{:S(2)}, u32[]{:S(2)}) collective-permute-start(bf16[768,256]{1,0:T(8,128)(2,1)} %collective-permute-done.63.refs_3_), channel_id=1, source_target_pairs={{0,4},{4,0},{1,5},{5,1},{2,6},{6,2},{3,7},{7,3},{8,12},{12,8},{9,1... | collective-permute-start | bytes 1179656 | tf_op jit(solution)/shard_map/ppermute | solution.py:394
  446.7 110.8 %all-gather.7.cloned.1.call-start = ((), (), s32[]{:S(2)}) async-start(), calls=%async_computation.8 | async-start | bytes 2785280 | tf_op jit(solution)/shard_map/all_gather | solution.py:805
  510.2 174.0 %reduce-scatter.11.cloned.1.call-start = ((), (), s32[]{:S(2)}) async-start(), calls=%async_computation.10 | async-start | bytes 2621440 | tf_op jit(solution)/shard_map/reduce_scatter | solution.py:840
  582.7 105.5 %reduce-scatter.9.cloned.1.call-start = ((), (), s32[]{:S(2)}) async-start(), calls=%async_computation.7 | async-start | bytes 2621440 | tf_op jit(solution)/shard_map/reduce_scatter | solution.py:813
  592.2 50.0 %collective-permute-start.118 = (bf16[1408,512]{1,0:T(8,128)(2,1)}, bf16[1408,512]{1,0:T(8,128)(2,1)}, u32[]{:S(2)}, u32[]{:S(2)}) collective-permute-start(bf16[1408,512]{1,0:T(8,128)(2,1)} %slice.532), channel_id=1, source_target_pairs={{0,16},{8,24},{16,0},{24,8},{1,17},{9,25},{17,1},{25,9},{2,18},{10... | collective-permute-start | bytes 4325384 | tf_op jit(solution)/shard_map/ppermute | solution.py:390
  595.0 63.8 %collective-permute-start.115 = (bf16[512,1536]{1,0:T(8,128)(2,1)}, bf16[512,1536]{1,0:T(8,128)(2,1)}, u32[]{:S(2)}, u32[]{:S(2)}) collective-permute-start(bf16[512,1536]{1,0:T(8,128)(2,1)} %slice.529), channel_id=1, source_target_pairs={{0,16},{8,24},{16,0},{24,8},{1,17},{9,25},{17,1},{25,9},{2,18},{10... | collective-permute-start | bytes 4718600 | tf_op jit(solution)/shard_map/ppermute | solution.py:390
  610.1 56.6 %collective-permute-start.84 = (bf16[1024,1408]{1,0:T(8,128)(2,1)}, bf16[1024,1408]{1,0:T(8,128)(2,1)}, u32[]{:S(2)}, u32[]{:S(2)}) collective-permute-start(bf16[1024,1408]{1,0:T(8,128)(2,1)} %convolution_convert_fusion.1), channel_id=1, source_target_pairs={{0,8},{8,0},{16,24},{24,16},{1,9},{9,1},{17,25},{25,17},{2,10},{10... | collective-permute-start | bytes 8650760 | tf_op jit(solution)/shard_map/ppermute | solution.py:386
  617.3 56.6 %collective-permute-start.85 = (bf16[1024,1408]{1,0:T(8,128)(2,1)}, bf16[1024,1408]{1,0:T(8,128)(2,1)}, u32[]{:S(2)}, u32[]{:S(2)}) collective-permute-start(bf16[1024,1408]{1,0:T(8,128)(2,1)} %convolution_convert_fusion), channel_id=1, source_target_pairs={{0,8},{8,0},{16,24},{24,16},{1,9},{9,1},{17,25},{25,17},{2,10},{10... | collective-permute-start | bytes 8650760 | tf_op jit(solution)/shard_map/ppermute | solution.py:386
  623.4 283.6 %all-gather.9.cloned.1.call-start = ((), (), s32[]{:S(2)}) async-start(), calls=%async_computation.9 | async-start | bytes 2621440 | tf_op jit(solution)/shard_map/all_gather | solution.py:882
  642.2 64.8 %collective-permute-start.107 = (bf16[512,1408]{1,0:T(8,128)(2,1)}, bf16[512,1408]{1,0:T(8,128)(2,1)}, u32[]{:S(2)}, u32[]{:S(2)}) collective-permute-start(bf16[512,1408]{1,0:T(8,128)(2,1)} %slice.521), channel_id=1, source_target_pairs={{0,4},{4,0},{1,5},{5,1},{2,6},{6,2},{3,7},{7,3},{8,12},{12,8},{9,1... | collective-permute-start | bytes 4325384 | tf_op jit(solution)/shard_map/ppermute | solution.py:394
  658.8 48.3 %collective-permute-start.108 = (bf16[512,1408]{1,0:T(8,128)(2,1)}, bf16[512,1408]{1,0:T(8,128)(2,1)}, u32[]{:S(2)}, u32[]{:S(2)}) collective-permute-start(bf16[512,1408]{1,0:T(8,128)(2,1)} %slice.522), channel_id=1, source_target_pairs={{0,16},{8,24},{16,0},{24,8},{1,17},{9,25},{17,1},{25,9},{2,18},{10... | collective-permute-start | bytes 4325384 | tf_op jit(solution)/shard_map/ppermute | solution.py:390
  695.4 214.7 %all-gather.11.cloned.1.call-start = ((), (), s32[]{:S(2)}) async-start(), calls=%async_computation.11 | async-start | bytes 2621440 | tf_op jit(solution)/shard_map/all_gather | solution.py:878
  757.4 55.9 %collective-permute-start.119 = (bf16[1408,256]{1,0:T(8,128)(2,1)S(1)}, bf16[1408,256]{1,0:T(8,128)(2,1)S(1)}, u32[]{:S(2)}, u32[]{:S(2)}) collective-permute-start(bf16[1408,256]{1,0:T(8,128)(2,1)S(1)} %copy-done.66), channel_id=1, source_target_pairs={{0,16},{8,24},{16,0},{24,8},{1,17},{9,25},{17,1},{25,9},{2,18},{10... | collective-permute-start | bytes 2162696 | tf_op jit(solution)/shard_map/ppermute | solution.py:390
  762.3 53.3 %collective-permute-start.102 = (bf16[1024,576]{0,1:T(8,128)(2,1)S(1)}, bf16[1024,576]{0,1:T(8,128)(2,1)}, u32[]{:S(2)}, u32[]{:S(2)}) collective-permute-start(bf16[1024,576]{0,1:T(8,128)(2,1)S(1)} %convolution_convert_fusion.20), channel_id=1, source_target_pairs={{0,8},{8,0},{16,24},{24,16},{1,9},{9,1},{17,25},{25,17},{2,10},{10... | collective-permute-start | bytes 3538952 | tf_op jit(solution)/shard_map/ppermute | solution.py:386
  815.6 50.5 %collective-permute-start.113 = (bf16[256,1408]{1,0:T(8,128)(2,1)}, bf16[256,1408]{1,0:T(8,128)(2,1)}, u32[]{:S(2)}, u32[]{:S(2)}) collective-permute-start(bf16[256,1408]{1,0:T(8,128)(2,1)} %add_convert_fusion.19), channel_id=1, source_target_pairs={{0,4},{4,0},{1,5},{5,1},{2,6},{6,2},{3,7},{7,3},{8,12},{12,8},{9,1... | collective-permute-start | bytes 2162696 | tf_op jit(solution)/shard_map/ppermute | solution.py:394
  820.4 46.9 %collective-permute-start.114 = (bf16[256,1408]{1,0:T(8,128)(2,1)}, bf16[256,1408]{1,0:T(8,128)(2,1)}, u32[]{:S(2)}, u32[]{:S(2)}) collective-permute-start(bf16[256,1408]{1,0:T(8,128)(2,1)} %add_convert_fusion.18), channel_id=1, source_target_pairs={{0,16},{8,24},{16,0},{24,8},{1,17},{9,25},{17,1},{25,9},{2,18},{10... | collective-permute-start | bytes 2162696 | tf_op jit(solution)/shard_map/ppermute | solution.py:390
  835.1 66.3 %collective-permute-start.103 = (bf16[512,576]{0,1:T(8,128)(2,1)}, bf16[512,576]{0,1:T(8,128)(2,1)}, u32[]{:S(2)}, u32[]{:S(2)}) collective-permute-start(bf16[512,576]{0,1:T(8,128)(2,1)} %copy.147), channel_id=1, source_target_pairs={{0,16},{8,24},{16,0},{24,8},{1,17},{9,25},{17,1},{25,9},{2,18},{10... | collective-permute-start | bytes 1769480 | tf_op jit(solution)/shard_map/ppermute | solution.py:390
  (254 other events, 3654.8 us)
Sparse Core Ops, SparseCore 0:
  117.6 42.9 reduce-scatter.4
  227.1 46.8 all-gather.4
  446.8 46.6 reduce-scatter.6
  510.4 47.0 all-gather.6
  582.8 42.3 reduce-scatter.10
  627.4 42.8 reduce-scatter.8
  695.5 55.6 all-gather.8
  752.7 44.5 all-gather.10
where the time goes:
time: 937 us; the launch traced here: 924 us
  waiting for transfers between devices  329 us (35%)
  matrix products  223 us (24%)
  Pallas kernels  134 us (14%)
  starting transfers between devices  84.7 us (9%)
  other arithmetic  73.4 us (8%)
  local copies, waits for them, and re-layouts  62.8 us (7%)
  between operations  16.6 us (2%)
    ppermute x31, waiting for transfers between devices, over_x(): return lax.ppermute(values, 'ctx', [(0, 1), (1, 0)])  177 us
    dot_general x28, matrix products, dot_tn(): lax.dot_general(left_in, right_in, (((0,), (0,)), ((), ())), preferred_el...  89.6 us
    ppermute x29, waiting for transfers between devices, over_y(): return lax.ppermute(values, 'dp', [(i, i ^ 2) for i in range(4)])  79.8 us
    dot_general x15, matrix products, dot_nn(): lax.dot_general(left_in, right_in, (((1,), (0,)), ((), ())), preferred_el...  71 us
    dot_general x13, matrix products, dot_nt(): lax.dot_general(left_in, right_in, (((1,), (1,)), ((), ())), preferred_el...  63 us
    ppermute x31, starting transfers between devices, over_x(): return lax.ppermute(values, 'ctx', [(0, 1), (1, 0)])  34.3 us
    all_gather x1, waiting for transfers between devices, local(): mixed_all = lax.all_gather(mixed_part, 'mp', axis=0, tiled=True)  34.3 us
    pallas_call x5, Pallas kernels, join_rows(): pl.pallas_call(body, out_shape=[shape] * experts, grid=(rows // tile,), i...  31.5 us
  transfers between devices with their start and end apart: 131, of which 44 were waited for; matrix products, arithmetic and copies ran while one was open for 32% of the time, Pallas kernels for 11%

commit v1 on v0

--- a/solution.py
+++ b/solution.py
@@ -692,9 +692,7 @@
     both_hot = jnp.concatenate(one_hot, axis=1)
     g_slots = [dot_tn(v, g_low).astype(BF16) for v in one_hot]
     down_near = [plan.tie(v, attn_part) for v in down_near]
-    down_full = [plan.collect(DOWN, down_shards[0], down_near[0], 1, True, *g_slots)]
-    act_back = [dot_nt(g_slots[0], down_full[0]).astype(BF16)]
-    attn_sum = plan.tie(attn_sum, act_back, *g_slots)
+    attn_sum = plan.tie(attn_sum, *g_slots)
     up_shard = plan.tie(expert_up, attn_part)
     up_near = plan.spread(up_shard)
     shared_gate, shared_up, shared_down = plan.tie((shared_gate, shared_up, shared_down), *g_slots)
@@ -714,8 +712,8 @@
     gate_joined, gate_rest = plan.collect(GATE, gate_shard, gate_near, 1, True)
     up_near = plan.tie(up_near, gate_joined)
     up_joined, up_rest = plan.collect(UP, up_shard, up_near, 1, False)
-    after = up_joined
-    for e in range(1, experts_here):
+    after, down_full, act_back = up_joined, [], []
+    for e in range(experts_here):
         full = plan.collect(DOWN, down_shards[e], down_near[e], 1, e % 2 == 0, after)
         down_full.append(full)
         act_back.append(dot_nt(g_slots[e], full).astype(BF16))
@@ -882,7 +880,8 @@
     result = lax.all_gather(result_own, "mp", axis=0, tiled=True)
 
     h_tail, heads_tail, low_tail, q_tail, comp_tail, pairs_tail = plan.tie(
-        (h_one, heads_flat, grad_low, grad_q_raw, comp_all, grad_pairs), input_own
+        (h_one, heads_flat, grad_low, grad_q_raw, comp_all, grad_pairs),
+        [g["held"] for g in sums_three],
     )
     sums_four = [
         plan.begin(FOUR, heads_tail, low_tail, block, 1, True),

time: 937 us -> 949 us (1.013)
    ppermute x31, waiting for transfers between devices: 177 us -> 146 us  [over_x(): return lax.ppermute(values, 'ctx', [(0, 1), (1, 0)])]
    reduce_scatter x1, waiting for transfers between devices: 0.01 us -> 29.7 us  [local(): lax.psum_scatter(attn_part, 'mp', scatter_dimension=0, tiled=True)]
    unnamed x304 -> x296, local copies, waits for them, and re-layouts: 19.9 us -> 23 us
  transfers between devices with their start and end apart: 131 -> 131, of which waited for: 44 -> 44; matrix products, arithmetic and copies ran while one was open for 32% -> 31% of each run, Pallas kernels for 11% -> 11%
where the time goes in v1:
time: 949 us; the launch traced here: 936 us
  waiting for transfers between devices  330 us (35%)
  matrix products  226 us (24%)
  Pallas kernels  134 us (14%)
  starting transfers between devices  89.7 us (9%)
  other arithmetic  75.4 us (8%)
  local copies, waits for them, and re-layouts  65 us (7%)
  between operations  16.7 us (2%)
    ppermute x31, waiting for transfers between devices, over_x(): return lax.ppermute(values, 'ctx', [(0, 1), (1, 0)])  146 us
    dot_general x28, matrix products, dot_tn(): lax.dot_general(left_in, right_in, (((0,), (0,)), ((), ())), preferred_el...  90.1 us
    ppermute x29, waiting for transfers between devices, over_y(): return lax.ppermute(values, 'dp', [(i, i ^ 2) for i in range(4)])  85.3 us
    dot_general x15, matrix products, dot_nn(): lax.dot_general(left_in, right_in, (((1,), (0,)), ((), ())), preferred_el...  71.3 us
    dot_general x13, matrix products, dot_nt(): lax.dot_general(left_in, right_in, (((1,), (1,)), ((), ())), preferred_el...  64.1 us
    ppermute x31, starting transfers between devices, over_x(): return lax.ppermute(values, 'ctx', [(0, 1), (1, 0)])  34.9 us
    all_gather x1, waiting for transfers between devices, local(): mixed_all = lax.all_gather(mixed_part, 'mp', axis=0, tiled=True)  34.3 us
    pallas_call x5, Pallas kernels, join_rows(): pl.pallas_call(body, out_shape=[shape] * experts, grid=(rows // tile,), i...  31.4 us
  transfers between devices with their start and end apart: 131, of which 44 were waited for; matrix products, arithmetic and copies ran while one was open for 31% of the time, Pallas kernels for 11%

profile of v1, /device:TPU:0, one launch (start us, length us, event | category | flops | bytes accessed | tf_op | source)
XLA Modules:
  0.0 936.3 jit_solution(16729331967891818271)
XLA Ops:
  66.1 9.1 collective-permute-done.20.refs_2_
  103.4 9.6 %shard_map.301 = (bf16[4,512,1024]{2,1,0:T(8,128)(2,1)}, bf16[512,512]{1,0:T(8,128)(2,1)}) custom-call(bf16[512,512]{1,0:T(8,128)(2,1)} %slice.702.plain_ref, bf16[512,256]{1,0:T(8,128)(2,1)} %pad_maximum_fusion.9.turned_ref, bf16[1024,1024]{1,0:T(8,128)(2,1)} %convolution_convert_fusion.17.pairs_ref, bf16[1024,64]{1,0:T(8,128)(2,1)} %maximum_bitcast_fusion.rope_ref, ...), custom_call_target="tpu_custom_call" | custom-call | flops 2147483648 | bytes 7077888 | tf_op jit(solution)/shard_map/pallas_call | solution.py:270
  130.8 29.7 %reduce-scatter.5.cloned.1.call-done = bf16[128,2048]{1,0:T(8,128)(2,1)} async-done(((bf16[512,2048]{1,0:T(8,128)(2,1)}), bf16[128,2048]{1,0:T(8,128)(2,1)}) %reduce-scatter.5.cloned.1.call-update) | async-done | bytes 524304 | tf_op jit(solution)/shard_map/reduce_scatter | solution.py:678
  172.5 9.6 %shard_map.304 = (bf16[8,256,1408]{2,1,0:T(8,128)(2,1)}, bf16[8,256,1408]{2,1,0:T(8,128)(2,1)}) custom-call(bf16[2,256,1408]{2,1,0:T(8,128)(2,1)} %refs_0_.4, bf16[2,256,1408]{2,1,0:T(8,128)(2,1)} %collective-permute-done.37.refs_1_, bf16[2,256,1408]{2,1,0:T(8,128)(2,1)} %collective-permute-done.38.refs_2_, bf16[2,256,1408]{2,1,0:T(8,128)(2,1)} %copy-done.61, ...), custom_call_target="tpu_custom_call" | custom-call | bytes 17301504 | tf_op jit(solution)/shard_map/pallas_call | solution.py:218
  182.2 17.7 %collective-permute-done.35.refs_1_ = bf16[2,256,1408]{2,1,0:T(8,128)(2,1)} collective-permute-done((bf16[2,256,1408]{2,1,0:T(8,128)(2,1)}, bf16[2,256,1408]{2,1,0:T(8,128)(2,1)}, u32[]{:S(2)}, u32[]{:S(2)}) %collective-permute-start.35) | collective-permute-done | bytes 1441824 | tf_op jit(solution)/shard_map/ppermute | solution.py:394
  201.8 12.9 %collective-permute-done.32.refs_1_ = bf16[1408,256]{1,0:T(8,128)(2,1)} collective-permute-done((bf16[1408,256]{1,0:T(8,128)(2,1)S(1)}, bf16[1408,256]{1,0:T(8,128)(2,1)}, u32[]{:S(2)}, u32[]{:S(2)}) %collective-permute-start.32) | collective-permute-done | bytes 720928 | tf_op jit(solution)/shard_map/ppermute | solution.py:394
  221.7 9.6 %shard_map.305 = (bf16[8,256,1408]{2,1,0:T(8,128)(2,1)}, bf16[8,256,1408]{2,1,0:T(8,128)(2,1)}) custom-call(bf16[2,256,1408]{2,1,0:T(8,128)(2,1)} %refs_0_.5, bf16[2,256,1408]{2,1,0:T(8,128)(2,1)} %collective-permute-done.35.refs_1_, bf16[2,256,1408]{2,1,0:T(8,128)(2,1)} %collective-permute-done.36.refs_2_, bf16[2,256,1408]{2,1,0:T(8,128)(2,1)} %copy-done.59, ...), custom_call_target="tpu_custom_call" | custom-call | bytes 17301504 | tf_op jit(solution)/shard_map/pallas_call | solution.py:218
  235.3 13.8 %collective-permute-done.51.refs_1_ = bf16[1408,256]{1,0:T(8,128)(2,1)} collective-permute-done((bf16[1408,256]{1,0:T(8,128)(2,1)S(1)}, bf16[1408,256]{1,0:T(8,128)(2,1)}, u32[]{:S(2)}, u32[]{:S(2)}) %collective-permute-start.51) | collective-permute-done | bytes 720928 | tf_op jit(solution)/shard_map/ppermute | solution.py:394
  276.9 7.9 convolution_convert_fusion.9
  284.8 17.5 %collective-permute-done.50.refs_0_ = bf16[2,256,1408]{2,1,0:T(8,128)(2,1)} collective-permute-done((bf16[2,256,1408]{2,1,0:T(8,128)(2,1)}, bf16[2,256,1408]{2,1,0:T(8,128)(2,1)}, u32[]{:S(2)}, u32[]{:S(2)}) %collective-permute-start.50) | collective-permute-done | bytes 1441824 | tf_op jit(solution)/shard_map/ppermute | solution.py:394
  314.7 8.4 fusion.162
  328.1 9.0 collective-permute-done.49.refs_0_
  344.8 22.2 %collective-permute-done.62.refs_1_ = bf16[768,256]{1,0:T(8,128)(2,1)S(1)} collective-permute-done((bf16[768,256]{1,0:T(8,128)(2,1)S(1)}, bf16[768,256]{1,0:T(8,128)(2,1)S(1)}, u32[]{:S(2)}, u32[]{:S(2)}) %collective-permute-start.62) | collective-permute-done | bytes 393248 | tf_op jit(solution)/shard_map/ppermute | solution.py:394
  376.4 8.4 fusion.26
  464.2 10.4 %collective-permute-done.75 = bf16[768,1024]{1,0:T(8,128)(2,1)S(1)} collective-permute-done((bf16[768,1024]{1,0:T(8,128)(2,1)S(1)}, bf16[768,1024]{1,0:T(8,128)(2,1)S(1)}, u32[]{:S(2)}, u32[]{:S(2)}) %collective-permute-start.75) | collective-permute-done | bytes 1572896 | tf_op jit(solution)/shard_map/ppermute | solution.py:386
  486.9 10.5 %reduce-scatter.7.cloned.1.call-done = bf16[128,2176]{1,0:T(8,128)(2,1)} async-done(((bf16[512,2176]{1,0:T(8,128)(2,1)}), bf16[128,2176]{1,0:T(8,128)(2,1)}) %reduce-scatter.7.cloned.1.call-update) | async-done | bytes 557072 | tf_op jit(solution)/shard_map/reduce_scatter | solution.py:779
  526.8 34.3 %all-gather.7.cloned.1.call-done = bf16[512,2176]{1,0:T(8,128)(2,1)} async-done(((bf16[128,2176]{1,0:T(8,128)(2,1)}), bf16[512,2176]{1,0:T(8,128)(2,1)}) %all-gather.7.cloned.1.call-update) | async-done | bytes 2228240 | tf_op jit(solution)/shard_map/all_gather | solution.py:803
  565.4 12.8 %shard_map.313 = (bf16[512,512]{1,0:T(8,128)(2,1)}, f32[512,256]{1,0:T(8,128)}, bf16[1024,1024]{1,0:T(8,128)(2,1)}, f32[1024,64]{1,0:T(8,128)}) custom-call(bf16[512,512]{1,0:T(8,128)(2,1)} %slice.702.plain_ref, bf16[512,256]{1,0:T(8,128)(2,1)} %pad_maximum_fusion.9.turned_ref, bf16[1024,1024]{1,0:T(8,128)(2,1)} %convolution_convert_fusion.17.pairs_ref, ...), custom_call_target="tpu_custom_call" | custom-call | flops 2684354560 | bytes 9961472 | tf_op jit(solution)/shard_map/pallas_call | solution.py:332
  645.5 20.1 %collective-permute-done.115.here_ref = bf16[512,1536]{1,0:T(8,128)(2,1)} collective-permute-done((bf16[512,1536]{1,0:T(8,128)(2,1)}, bf16[512,1536]{1,0:T(8,128)(2,1)}, u32[]{:S(2)}, u32[]{:S(2)}) %collective-permute-start.115) | collective-permute-done | bytes 1572896 | tf_op jit(solution)/shard_map/ppermute | solution.py:390
  677.9 8.3 collective-permute-done.80
  783.1 11.6 %collective-permute-done.111.refs_1_ = bf16[512,1408]{1,0:T(8,128)(2,1)} collective-permute-done((bf16[512,1408]{1,0:T(8,128)(2,1)}, bf16[512,1408]{1,0:T(8,128)(2,1)}, u32[]{:S(2)}, u32[]{:S(2)}) %collective-permute-start.111) | collective-permute-done | bytes 1441824 | tf_op jit(solution)/shard_map/ppermute | solution.py:390
  805.3 9.8 %collective-permute-done.94.refs_1_ = bf16[512,512]{1,0:T(8,128)(2,1)S(1)} collective-permute-done((bf16[512,512]{1,0:T(8,128)(2,1)S(1)}, bf16[512,512]{1,0:T(8,128)(2,1)S(1)}, u32[]{:S(2)}, u32[]{:S(2)}) %collective-permute-start.94) | collective-permute-done | bytes 524320 | tf_op jit(solution)/shard_map/ppermute | solution.py:394
  816.6 8.6 collective-permute-done.95.refs_1_
  864.8 13.6 %collective-permute-done.113.refs_2_ = bf16[256,1408]{1,0:T(8,128)(2,1)} collective-permute-done((bf16[256,1408]{1,0:T(8,128)(2,1)}, bf16[256,1408]{1,0:T(8,128)(2,1)}, u32[]{:S(2)}, u32[]{:S(2)}) %collective-permute-start.113) | collective-permute-done | bytes 720928 | tf_op jit(solution)/shard_map/ppermute | solution.py:394
  (782 shorter events, 594.2 us)
Async XLA Ops:
  7.2 153.3 %reduce-scatter.5.cloned.1.call-start = ((), (), s32[]{:S(2)}) async-start(), calls=%async_computation.4 | async-start | bytes 2621440 | tf_op jit(solution)/shard_map/reduce_scatter | solution.py:678
  117.4 186.9 %all-gather.5.cloned.1.call-start = ((), (), s32[]{:S(2)}) async-start(), calls=%async_computation.5 | async-start | bytes 2621440 | tf_op jit(solution)/shard_map/all_gather | solution.py:709
  249.6 247.7 %reduce-scatter.7.cloned.1.call-start = ((), (), s32[]{:S(2)}) async-start(), calls=%async_computation.6 | async-start | bytes 2785280 | tf_op jit(solution)/shard_map/reduce_scatter | solution.py:779
  367.0 53.9 %collective-permute-start.65 = (bf16[256,1536]{1,0:T(8,128)(2,1)}, bf16[256,1536]{1,0:T(8,128)(2,1)}, u32[]{:S(2)}, u32[]{:S(2)}) collective-permute-start(bf16[256,1536]{1,0:T(8,128)(2,1)} %get-tuple-element.364), channel_id=1, source_target_pairs={{0,8},{8,0},{16,24},{24,16},{1,9},{9,1},{17,25},{25,17},{2,10},{10... | collective-permute-start | bytes 2359304 | tf_op jit(solution)/shard_map/ppermute | solution.py:386
  368.9 52.5 %collective-permute-start.66 = (bf16[256,1536]{1,0:T(8,128)(2,1)}, bf16[256,1536]{1,0:T(8,128)(2,1)}, u32[]{:S(2)}, u32[]{:S(2)}) collective-permute-start(bf16[256,1536]{1,0:T(8,128)(2,1)} %collective-permute-done.60), channel_id=1, source_target_pairs={{0,8},{8,0},{16,24},{24,16},{1,9},{9,1},{17,25},{25,17},{2,10},{10... | collective-permute-start | bytes 2359304 | tf_op jit(solution)/shard_map/ppermute | solution.py:386
  368.9 52.6 %collective-permute-start.68 = (bf16[256,1536]{1,0:T(8,128)(2,1)}, bf16[256,1536]{1,0:T(8,128)(2,1)}, u32[]{:S(2)}, u32[]{:S(2)}) collective-permute-start(bf16[256,1536]{1,0:T(8,128)(2,1)} %collective-permute-done.61), channel_id=1, source_target_pairs={{0,8},{8,0},{16,24},{24,16},{1,9},{9,1},{17,25},{25,17},{2,10},{10... | collective-permute-start | bytes 2359304 | tf_op jit(solution)/shard_map/ppermute | solution.py:386
  371.8 56.0 %collective-permute-start.69 = (bf16[768,256]{1,0:T(8,128)(2,1)}, bf16[768,256]{1,0:T(8,128)(2,1)}, u32[]{:S(2)}, u32[]{:S(2)}) collective-permute-start(bf16[768,256]{1,0:T(8,128)(2,1)} %collective-permute-done.63.refs_3_), channel_id=1, source_target_pairs={{0,4},{4,0},{1,5},{5,1},{2,6},{6,2},{3,7},{7,3},{8,12},{12,8},{9,1... | collective-permute-start | bytes 1179656 | tf_op jit(solution)/shard_map/ppermute | solution.py:394
  453.9 107.2 %all-gather.7.cloned.1.call-start = ((), (), s32[]{:S(2)}) async-start(), calls=%async_computation.8 | async-start | bytes 2785280 | tf_op jit(solution)/shard_map/all_gather | solution.py:803
  513.8 207.9 %reduce-scatter.11.cloned.1.call-start = ((), (), s32[]{:S(2)}) async-start(), calls=%async_computation.10 | async-start | bytes 2621440 | tf_op jit(solution)/shard_map/reduce_scatter | solution.py:838
  586.3 139.6 %reduce-scatter.9.cloned.1.call-start = ((), (), s32[]{:S(2)}) async-start(), calls=%async_computation.7 | async-start | bytes 2621440 | tf_op jit(solution)/shard_map/reduce_scatter | solution.py:811
  596.5 47.7 %collective-permute-start.117 = (bf16[1408,512]{1,0:T(8,128)(2,1)}, bf16[1408,512]{1,0:T(8,128)(2,1)}, u32[]{:S(2)}, u32[]{:S(2)}) collective-permute-start(bf16[1408,512]{1,0:T(8,128)(2,1)} %slice.531), channel_id=1, source_target_pairs={{0,4},{4,0},{1,5},{5,1},{2,6},{6,2},{3,7},{7,3},{8,12},{12,8},{9,1... | collective-permute-start | bytes 4325384 | tf_op jit(solution)/shard_map/ppermute | solution.py:394
  597.1 48.4 %collective-permute-start.118 = (bf16[1408,512]{1,0:T(8,128)(2,1)}, bf16[1408,512]{1,0:T(8,128)(2,1)}, u32[]{:S(2)}, u32[]{:S(2)}) collective-permute-start(bf16[1408,512]{1,0:T(8,128)(2,1)} %slice.532), channel_id=1, source_target_pairs={{0,16},{8,24},{16,0},{24,8},{1,17},{9,25},{17,1},{25,9},{2,18},{10... | collective-permute-start | bytes 4325384 | tf_op jit(solution)/shard_map/ppermute | solution.py:390
  599.7 65.9 %collective-permute-start.115 = (bf16[512,1536]{1,0:T(8,128)(2,1)}, bf16[512,1536]{1,0:T(8,128)(2,1)}, u32[]{:S(2)}, u32[]{:S(2)}) collective-permute-start(bf16[512,1536]{1,0:T(8,128)(2,1)} %slice.529), channel_id=1, source_target_pairs={{0,16},{8,24},{16,0},{24,8},{1,17},{9,25},{17,1},{25,9},{2,18},{10... | collective-permute-start | bytes 4718600 | tf_op jit(solution)/shard_map/ppermute | solution.py:390
  617.6 306.8 %all-gather.9.cloned.1.call-start = ((), (), s32[]{:S(2)}) async-start(), calls=%async_computation.9 | async-start | bytes 2621440 | tf_op jit(solution)/shard_map/all_gather | solution.py:880
  622.9 67.3 %collective-permute-start.107 = (bf16[512,1408]{1,0:T(8,128)(2,1)}, bf16[512,1408]{1,0:T(8,128)(2,1)}, u32[]{:S(2)}, u32[]{:S(2)}) collective-permute-start(bf16[512,1408]{1,0:T(8,128)(2,1)} %slice.521), channel_id=1, source_target_pairs={{0,4},{4,0},{1,5},{5,1},{2,6},{6,2},{3,7},{7,3},{8,12},{12,8},{9,1... | collective-permute-start | bytes 4325384 | tf_op jit(solution)/shard_map/ppermute | solution.py:394
  639.8 54.6 %collective-permute-start.108 = (bf16[512,1408]{1,0:T(8,128)(2,1)}, bf16[512,1408]{1,0:T(8,128)(2,1)}, u32[]{:S(2)}, u32[]{:S(2)}) collective-permute-start(bf16[512,1408]{1,0:T(8,128)(2,1)} %slice.522), channel_id=1, source_target_pairs={{0,16},{8,24},{16,0},{24,8},{1,17},{9,25},{17,1},{25,9},{2,18},{10... | collective-permute-start | bytes 4325384 | tf_op jit(solution)/shard_map/ppermute | solution.py:390
  645.5 55.6 %collective-permute-start.84 = (bf16[1024,1408]{1,0:T(8,128)(2,1)}, bf16[1024,1408]{1,0:T(8,128)(2,1)}, u32[]{:S(2)}, u32[]{:S(2)}) collective-permute-start(bf16[1024,1408]{1,0:T(8,128)(2,1)} %convolution_convert_fusion.1), channel_id=1, source_target_pairs={{0,8},{8,0},{16,24},{24,16},{1,9},{9,1},{17,25},{25,17},{2,10},{10... | collective-permute-start | bytes 8650760 | tf_op jit(solution)/shard_map/ppermute | solution.py:386
  732.8 191.6 %all-gather.11.cloned.1.call-start = ((), (), s32[]{:S(2)}) async-start(), calls=%async_computation.11 | async-start | bytes 2621440 | tf_op jit(solution)/shard_map/all_gather | solution.py:876
  768.9 72.0 %collective-permute-start.119 = (bf16[1408,256]{1,0:T(8,128)(2,1)}, bf16[1408,256]{1,0:T(8,128)(2,1)}, u32[]{:S(2)}, u32[]{:S(2)}) collective-permute-start(bf16[1408,256]{1,0:T(8,128)(2,1)} %add_convert_fusion.17), channel_id=1, source_target_pairs={{0,16},{8,24},{16,0},{24,8},{1,17},{9,25},{17,1},{25,9},{2,18},{10... | collective-permute-start | bytes 2162696 | tf_op jit(solution)/shard_map/ppermute | solution.py:390
  776.5 48.7 %collective-permute-start.95 = (bf16[512,768]{1,0:T(8,128)(2,1)S(1)}, bf16[512,768]{1,0:T(8,128)(2,1)S(1)}, u32[]{:S(2)}, u32[]{:S(2)}) collective-permute-start(bf16[512,768]{1,0:T(8,128)(2,1)S(1)} %slice.505), channel_id=1, source_target_pairs={{0,16},{8,24},{16,0},{24,8},{1,17},{9,25},{17,1},{25,9},{2,18},{10... | collective-permute-start | bytes 2359304 | tf_op jit(solution)/shard_map/ppermute | solution.py:390
  782.5 53.9 %collective-permute-start.102 = (bf16[1024,576]{0,1:T(8,128)(2,1)S(1)}, bf16[1024,576]{0,1:T(8,128)(2,1)}, u32[]{:S(2)}, u32[]{:S(2)}) collective-permute-start(bf16[1024,576]{0,1:T(8,128)(2,1)S(1)} %convolution_convert_fusion.20), channel_id=1, source_target_pairs={{0,8},{8,0},{16,24},{24,16},{1,9},{9,1},{17,25},{25,17},{2,10},{10... | collective-permute-start | bytes 3538952 | tf_op jit(solution)/shard_map/ppermute | solution.py:386
  841.7 53.5 %collective-permute-start.114 = (bf16[256,1408]{1,0:T(8,128)(2,1)}, bf16[256,1408]{1,0:T(8,128)(2,1)}, u32[]{:S(2)}, u32[]{:S(2)}) collective-permute-start(bf16[256,1408]{1,0:T(8,128)(2,1)} %add_convert_fusion.18), channel_id=1, source_target_pairs={{0,16},{8,24},{16,0},{24,8},{1,17},{9,25},{17,1},{25,9},{2,18},{10... | collective-permute-start | bytes 2162696 | tf_op jit(solution)/shard_map/ppermute | solution.py:390
  847.5 64.9 %collective-permute-start.103 = (bf16[512,576]{0,1:T(8,128)(2,1)}, bf16[512,576]{0,1:T(8,128)(2,1)}, u32[]{:S(2)}, u32[]{:S(2)}) collective-permute-start(bf16[512,576]{0,1:T(8,128)(2,1)} %copy.147), channel_id=1, source_target_pairs={{0,16},{8,24},{16,0},{24,8},{1,17},{9,25},{17,1},{25,9},{2,18},{10... | collective-permute-start | bytes 1769480 | tf_op jit(solution)/shard_map/ppermute | solution.py:390
  854.9 52.2 %collective-permute-start.98 = (bf16[256,768]{1,0:T(8,128)(2,1)}, bf16[256,768]{1,0:T(8,128)(2,1)S(1)}, u32[]{:S(2)}, u32[]{:S(2)}) collective-permute-start(bf16[256,768]{1,0:T(8,128)(2,1)} %add_convert_fusion.25), channel_id=1, source_target_pairs={{0,4},{4,0},{1,5},{5,1},{2,6},{6,2},{3,7},{7,3},{8,12},{12,8},{9,1... | collective-permute-start | bytes 1179656 | tf_op jit(solution)/shard_map/ppermute | solution.py:394
  (250 other events, 3859.6 us)
Sparse Core Ops, SparseCore 0:
  117.5 42.9 reduce-scatter.4
  249.8 43.9 all-gather.4
  454.0 43.2 reduce-scatter.6
  513.9 47.0 all-gather.6
  586.4 42.3 reduce-scatter.10
  631.0 42.8 reduce-scatter.8
  733.0 57.9 all-gather.8
  792.6 44.3 all-gather.10
